TPU v7x, 256 devices: a whole 4x4x8 slice. The times are simulated.
256 devices in a mesh: wide: 32 (over x, z_lo, core), narrow: 8 (over y, z_hi).
Axes of the slice: x: 4, y: 4, z: 8 (z_hi: 2, z_lo: 4; z = z_hi * 4 + z_lo), core: 2. Of those that a mesh axis runs over, the one named last changes fastest.
Arguments:
- hidden_in: bfloat16 [2048, 6144], P('wide', 'narrow'), may hold values from -6 to 6
- w_query: bfloat16 [6144, 6144], P('narrow', 'wide'), may hold values from -1 to 1
- w_key: bfloat16 [6144, 6144], P('narrow', 'wide'), may hold values from -1 to 1
- w_value: bfloat16 [6144, 6144], P('narrow', 'wide'), may hold values from -0.078125 to 0.078125
- qkv_bias: float32 [3, 6144], P(None, 'wide'), may hold values from -3 to 3
- w_up: bfloat16 [6144, 24576], P('narrow', 'wide'), may hold values from -0.078125 to 0.078125
- up_bias: float32 [24576], P('wide'), may hold values from -3 to 3
- w_attn_out: bfloat16 [6144, 6144], P('wide', 'narrow'), may hold values from -0.078125 to 0.078125
- w_down: bfloat16 [24576, 6144], P('wide', 'narrow'), may hold values from -0.0390625 to 0.0390625
- out_bias: float32 [6144], P('narrow'), may hold values from -3 to 3
- norm_gain: float32 [2, 6144], P(None, 'narrow'), may hold values from 0.5 to 1.5
- norm_bias: float32 [2, 6144], P(None, 'narrow'), may hold values from -2 to 2
- seq_lens: int32 [8], replicated, may hold values from 1 to 1024, 2048 in all
- sink_count: int32 [8], replicated, may hold values from 1 to 64, as said below
- page_table: int32 [128], replicated, may hold values from 0 to 127, each once
Outputs:
- hidden_out: bfloat16 [2048, 6144], P('wide', 'narrow')
- paged_cache: bfloat16 [2, 128, 16, 6144], P(None, 'narrow', None, 'wide')
Inputs may be any that keep to these rules, and one draw needn't show every extreme that they name: `seq_lens`: the lengths are positive, add up to 2048, and the longest is exactly 1024. `sink_count`: some sequence has exactly 64 sink tokens. `page_table`: every slot is named by exactly one page.
All inputs are finite; a program needn't handle non-finite values.
Results may differ from a plain program's by a relative error of at most 0.02.
Values may be sent and summed in bfloat16 or wider, within the bound.
A program may use at most 64 MiB of HBM per device.

v0:
```python
import jax
import jax.numpy as jnp
from jax import lax
from jax.sharding import PartitionSpec as P

D = 6144
HEAD_DIM = 96
ROTARY = 24
PAGE = 16


def segment_info(token_index, seq_lens, sink_count):
    seq_ends = jnp.cumsum(seq_lens)
    seq_starts = seq_ends - seq_lens
    inside = (token_index[:, None] >= seq_starts[None, :]) & (
        token_index[:, None] < seq_ends[None, :]
    )
    member = inside.astype(jnp.int32)
    seq_number = jnp.arange(seq_lens.shape[0], dtype=jnp.int32)
    segment = jnp.sum(member * seq_number[None, :], axis=1)
    position = token_index - jnp.sum(member * seq_starts[None, :], axis=1)
    sink_limit = jnp.sum(member * sink_count[None, :], axis=1)
    return (segment, position, sink_limit)


def rotate(values, position):
    half_rot = ROTARY // 2
    freq_index = jnp.arange(half_rot, dtype=jnp.float32)
    inverse = jnp.power(jnp.float32(10000.0), -2.0 * freq_index / ROTARY)
    angles = position.astype(jnp.float32)[:, None] * inverse[None, :]
    cosine = jnp.cos(angles)[:, None, :]
    sine_part = jnp.sin(angles)[:, None, :]
    first_half = values[..., :half_rot]
    second_half = values[..., half_rot:ROTARY]
    return jnp.concatenate(
        [
            first_half * cosine - second_half * sine_part,
            second_half * cosine + first_half * sine_part,
            values[..., ROTARY:],
        ],
        axis=-1,
    )


def local(
    hidden_in,
    w_query,
    w_key,
    w_value,
    qkv_bias,
    w_up,
    up_bias,
    w_attn_out,
    w_down,
    out_bias,
    norm_gain,
    norm_bias,
    seq_lens,
    sink_count,
    page_table,
):
    wide_count = lax.axis_size("wide")
    narrow_count = lax.axis_size("narrow")
    narrow_index = lax.axis_index("narrow")
    tok_local, feat_local = hidden_in.shape
    sub_rows = tok_local // narrow_count
    total_tokens = tok_local * wide_count
    query_rows = wide_count * sub_rows
    head_cols = w_query.shape[1]
    heads_local = head_cols // HEAD_DIM
    as_float = hidden_in.astype(jnp.float32)
    partial_sum = jnp.sum(as_float, axis=1)
    partial_square = jnp.sum(as_float * as_float, axis=1)
    total_sum, total_square = lax.psum((partial_sum, partial_square), "narrow")
    average = total_sum / D
    variance = total_square / D - average * average
    scaled = (as_float - average[:, None]) * lax.rsqrt(variance + 1e-05)[:, None]
    attn_normed = (scaled * norm_gain[0] + norm_bias[0]).astype(jnp.bfloat16)
    mlp_normed = (scaled * norm_gain[1] + norm_bias[1]).astype(jnp.bfloat16)
    stacked = jnp.stack([attn_normed, mlp_normed]).reshape(2, narrow_count, sub_rows, feat_local)
    gathered = lax.all_gather(stacked, "wide", axis=2, tiled=True).reshape(
        2, total_tokens, feat_local
    )
    local_order = jnp.arange(query_rows, dtype=jnp.int32)
    local_tokens = (
        local_order // sub_rows * tok_local + narrow_index * sub_rows + local_order % sub_rows
    )
    local_seg, local_pos, local_sink = segment_info(local_tokens, seq_lens, sink_count)
    all_order = jnp.arange(total_tokens, dtype=jnp.int32)
    all_tokens = (
        all_order % query_rows // sub_rows * tok_local
        + all_order // query_rows * sub_rows
        + all_order % sub_rows
    )
    all_seg, all_pos, all_sink = segment_info(all_tokens, seq_lens, sink_count)
    qkv_weight = jnp.concatenate([w_query, w_key, w_value], axis=1)
    attn_part = gathered[0]
    mlp_part = gathered[1]
    summed = lax.psum_scatter(
        jnp.concatenate(
            [
                jnp.dot(attn_part, qkv_weight, preferred_element_type=jnp.float32),
                jnp.dot(mlp_part, w_up, preferred_element_type=jnp.float32),
            ],
            axis=1,
        ).astype(jnp.bfloat16),
        "narrow",
        scatter_dimension=0,
        tiled=True,
    ).astype(jnp.float32)
    query_sum = summed[:, :head_cols]
    key_sum = summed[:, head_cols : 2 * head_cols]
    value_sum = summed[:, 2 * head_cols : 3 * head_cols]
    unit_sum = summed[:, 3 * head_cols :]
    keys_local = (
        rotate((key_sum + qkv_bias[1]).reshape(query_rows, heads_local, HEAD_DIM), local_pos)
        .astype(jnp.bfloat16)
        .reshape(query_rows, head_cols)
    )
    values_local = (value_sum + qkv_bias[2]).astype(jnp.bfloat16)
    all_keys, all_values = (
        lax.all_gather(keys_local, "narrow", axis=0, tiled=True),
        lax.all_gather(values_local, "narrow", axis=0, tiled=True),
    )
    queries = rotate(
        (query_sum + qkv_bias[0]).reshape(query_rows, heads_local, HEAD_DIM), local_pos
    ).astype(jnp.bfloat16)
    hidden_units = jax.nn.gelu(unit_sum + up_bias, approximate=False).astype(jnp.bfloat16)
    window_span = total_tokens // 16
    allowed = (local_seg[:, None] == all_seg[None, :]) & (all_pos[None, :] <= local_pos[:, None])
    allowed = allowed & (
        (local_pos[:, None] - all_pos[None, :] < window_span)
        | (all_pos[None, :] < local_sink[:, None])
    )
    key_heads = all_keys.reshape(total_tokens, heads_local, HEAD_DIM)
    value_heads = all_values.reshape(total_tokens, heads_local, HEAD_DIM)
    scores = jnp.einsum("qhd,khd->hqk", queries, key_heads, preferred_element_type=jnp.float32) * (
        1.0 / HEAD_DIM**0.5
    )
    masked = jnp.where(allowed[None], scores, jnp.float32(-1e30))
    top_score = jnp.max(masked, axis=2, keepdims=True)
    weights = jnp.exp(masked - top_score)
    probs = (weights / jnp.sum(weights, axis=2, keepdims=True)).astype(jnp.bfloat16)
    attended = (
        jnp.einsum("hqk,khd->qhd", probs, value_heads, preferred_element_type=jnp.float32)
        .astype(jnp.bfloat16)
        .reshape(query_rows, head_cols)
    )
    full_out, full_down = (
        lax.all_gather(w_attn_out, "narrow", axis=1, tiled=True),
        lax.all_gather(w_down, "narrow", axis=1, tiled=True),
    )
    attn_part = attended
    own_rows = lax.psum_scatter(
        (
            jnp.dot(attn_part, full_out, preferred_element_type=jnp.float32)
            + jnp.dot(hidden_units, full_down, preferred_element_type=jnp.float32)
        ).astype(jnp.bfloat16),
        "wide",
        scatter_dimension=0,
        tiled=True,
    ).astype(jnp.float32)
    combined = lax.all_to_all(
        own_rows.astype(jnp.bfloat16), "narrow", split_axis=1, concat_axis=0, tiled=True
    ).astype(own_rows.dtype)
    hidden_out = (as_float + combined + out_bias).astype(jnp.bfloat16)
    pages_local = page_table.shape[0] // narrow_count
    slot_ids = narrow_index * pages_local + jnp.arange(pages_local, dtype=jnp.int32)
    matches = (page_table[None, :] == slot_ids[:, None]).astype(jnp.int32)
    source_page = jnp.sum(
        matches * jnp.arange(page_table.shape[0], dtype=jnp.int32)[None, :], axis=1
    )
    token_ids = (source_page[:, None] * PAGE + jnp.arange(PAGE, dtype=jnp.int32)[None, :]).reshape(
        -1
    )
    gather_rows = (
        token_ids % tok_local // sub_rows * query_rows
        + token_ids // tok_local * sub_rows
        + token_ids % sub_rows
    )
    cache_keys = jnp.take(all_keys, gather_rows, axis=0).reshape(pages_local, PAGE, head_cols)
    cache_values = jnp.take(all_values, gather_rows, axis=0).reshape(pages_local, PAGE, head_cols)
    paged_cache = jnp.stack([cache_keys, cache_values])
    return (hidden_out, paged_cache)


def solution(mesh):
    in_specs = (
        P("wide", "narrow"),
        P("narrow", "wide"),
        P("narrow", "wide"),
        P("narrow", "wide"),
        P(None, "wide"),
        P("narrow", "wide"),
        P("wide"),
        P("wide", "narrow"),
        P("wide", "narrow"),
        P("narrow"),
        P(None, "narrow"),
        P(None, "narrow"),
        P(),
        P(),
        P(),
    )
    out_specs = (P("wide", "narrow"), P(None, "narrow", None, "wide"))
    return jax.shard_map(local, mesh=mesh, in_specs=in_specs, out_specs=out_specs, check_vma=False)
```

profile of v0, /device:TPU:8, one launch (start us, length us, event | category | flops | bytes accessed | tf_op | source)
XLA Modules:
  0.0 761.1 jit_solution(3944237115686412348)
XLA Ops:
  7.2 1.1 convert_reduce_fusion
  8.3 31.2 %all-reduce = (f32[64]{0:T(128)S(1)}, f32[64]{0:T(128)S(1)}) all-reduce(f32[64]{0:T(128)S(1)} %get-tuple-element.4, f32[64]{0:T(128)S(1)} %get-tuple-element.3), channel_id=1, replica_groups=mesh['wide'=32,'narrow'=8] {'narrow'}, use_global_device_ids=true, to_apply=%region_3.0 | all-reduce | flops 128 | bytes 1024 | tf_op jit(solution)/shard_map/psum | solution.py:74
  39.6 0.8 slice_reduce_fusion.2
  40.4 1.0 fusion.72
  41.4 0.7 pad_maximum_fusion.2
  42.2 63.7 %all-gather.4.cloned.1.call-done = bf16[2,8,256,768]{3,2,1,0:T(8,128)(2,1)} async-done(((bf16[2,8,8,768]{3,2,1,0:T(8,128)(2,1)}), bf16[2,8,256,768]{3,2,1,0:T(8,128)(2,1)}) %all-gather.4.cloned.1.call-update) | async-done | bytes 6291472 | tf_op jit(solution)/shard_map/all_gather | solution.py:81
  105.9 3.3 fusion.142
  109.2 2.9 convolution_convert_fusion
  112.2 2.0 convolution_convert_fusion.1
  114.2 2.9 pad_maximum_fusion
  117.2 0.7 all-gather.8.cloned.1.call-update
  119.2 0.9 fusion.6
  120.1 142.9 %reduce-scatter.3.cloned.1.call-done = bf16[256,1344]{0,1:T(8,128)(2,1)} async-done(((bf16[2048,1344]{0,1:T(8,128)(2,1)}), bf16[256,1344]{0,1:T(8,128)(2,1)}) %reduce-scatter.3.cloned.1.call-update) | async-done | bytes 688144 | tf_op jit(solution)/shard_map/reduce_scatter | solution.py:99
  262.9 1.2 convert_element_type.65
  264.1 1.1 copy-done.2
  265.2 0.8 slice_add_fusion.2
  267.4 76.0 %all_gather.17 = bf16[2048,192]{1,0:T(8,128)(2,1)S(1)} all-gather(bf16[256,192]{1,0:T(8,128)(2,1)S(1)} %copy.20), channel_id=1, replica_groups=mesh['wide'=32,'narrow'=8] {'narrow'}, dimensions={0}, use_global_device_ids=true | all-gather | bytes 884736 | tf_op jit(solution)/shard_map/all_gather | solution.py:122
  344.0 3.3 fusion.144
  347.2 65.6 %all_gather.16 = bf16[2048,192]{0,1:T(8,128)(2,1)S(1)} all-gather(bf16[256,192]{0,1:T(8,128)(2,1)} %get-tuple-element.24), channel_id=1, replica_groups=mesh['wide'=32,'narrow'=8] {'narrow'}, dimensions={0}, use_global_device_ids=true | all-gather | bytes 884736 | tf_op jit(solution)/shard_map/all_gather | solution.py:123
  412.9 4.1 fusion.9
  416.9 86.6 %all-gather.8.cloned.1.call-done = bf16[768,6144]{1,0:T(8,128)(2,1)} async-done(((bf16[768,768]{1,0:T(8,128)(2,1)}), bf16[768,6144]{1,0:T(8,128)(2,1)}) %all-gather.8.cloned.1.call-update) | async-done | bytes 9437200 | tf_op jit(solution)/shard_map/all_gather | solution.py:151
  503.5 11.0 %fusion.27 = f32[256,6144]{1,0:T(8,128)} fusion(bf16[768,6144]{1,0:T(8,128)(2,1)} %all-gather.8.cloned.1.call-done, f32[256,1344]{0,1:T(8,128)} %copy-done.2, f32[768]{0:T(1024)} %param.23), kind=kOutput, calls=%fused_computation.46 | convolution fusion | flops 2428895232 | bytes 16519168 | tf_op jit(solution)/shard_map/dot_general | solution.py:157
  514.6 70.8 %all-gather.6.cloned.1.call-done = bf16[192,6144]{1,0:T(8,128)(2,1)} async-done(((bf16[192,768]{1,0:T(8,128)(2,1)}), bf16[192,6144]{1,0:T(8,128)(2,1)}) %all-gather.6.cloned.1.call-update) | async-done | bytes 2359312 | tf_op jit(solution)/shard_map/all_gather | solution.py:150
  585.3 6.2 fusion.1
  592.6 1.4 copy.22
  594.0 1.2 gather_fusion
  595.2 1.2 gather_fusion.1
  596.3 141.5 %reduce-scatter.5.cloned.1.call-done = bf16[8,6144]{1,0:T(8,128)(2,1)} async-done(((bf16[256,6144]{1,0:T(8,128)(2,1)}), bf16[8,6144]{1,0:T(8,128)(2,1)}) %reduce-scatter.5.cloned.1.call-update) | async-done | bytes 98320 | tf_op jit(solution)/shard_map/reduce_scatter | solution.py:154
  737.9 7.2 all-to-all-start
  745.2 0.7 pad_maximum_fusion.1
  745.9 8.0 %all-to-all-done = bf16[8,8,768]{2,0,1:T(8,128)(2,1)S(1)} async-done(((bf16[8,8,768]{2,0,1:T(8,128)(2,1)}), bf16[8,8,768]{2,0,1:T(8,128)(2,1)S(1)}, u32[]{:S(2)}, u32[]{:S(2)}) %all-to-all-start) | async-done | bytes 98336 | tf_op jit(solution)/shard_map/all_to_all | solution.py:163
  753.9 0.7 fusion.69
  (62 shorter events, 4.4 us)
Async XLA Ops:
  7.2 102.0 %copy-start = (bf16[768,768]{1,0:T(8,128)(2,1)S(1)}, bf16[768,768]{1,0:T(8,128)(2,1)}, u32[]{:S(2)}) copy-start(bf16[768,768]{1,0:T(8,128)(2,1)} %param.22) | copy-start | bytes 3538948
  7.2 98.7 %all-gather.4.cloned.1.call-start = ((), (), s32[]{:S(2)}) async-start(), calls=%async_computation.3 | async-start | bytes 6488064 | tf_op jit(solution)/shard_map/all_gather | solution.py:81
  42.1 220.8 %reduce-scatter.3.cloned.1.call-start = ((), (), s32[]{:S(2)}) async-start(), calls=%async_computation.4 | async-start | bytes 6193152 | tf_op jit(solution)/shard_map/reduce_scatter | solution.py:99
  109.2 3.0 copy-start.9
  109.2 3.0 copy-start.10
  109.2 3.0 copy-start.11
  117.1 1.4 copy-start.12
  117.1 1.6 copy-start.8
  117.1 1.9 copy-start.7
  117.2 386.4 %all-gather.8.cloned.1.call-start = ((), (), s32[]{:S(2)}) async-start(), calls=%async_computation.6 | async-start | bytes 10616832 | tf_op jit(solution)/shard_map/all_gather | solution.py:151
  117.9 467.4 %all-gather.6.cloned.1.call-start = ((), (), s32[]{:S(2)}) async-start(), calls=%async_computation.5 | async-start | bytes 2654208 | tf_op jit(solution)/shard_map/all_gather | solution.py:150
  118.5 619.4 %reduce-scatter.5.cloned.1.call-start = ((), (), s32[]{:S(2)}) async-start(), calls=%async_computation.7 | async-start | bytes 3244032 | tf_op jit(solution)/shard_map/reduce_scatter | solution.py:154
  264.1 1.1 copy-start.2
  344.0 3.3 copy-start.4
  412.9 4.1 copy-start.1
  416.9 168.4 %copy-start.5 = (bf16[2,96,256]{2,1,0:T(8,128)(2,1)S(1)}, bf16[2,96,256]{2,1,0:T(8,128)(2,1)}, u32[]{:S(2)}) copy-start(bf16[2,96,256]{2,1,0:T(8,128)(2,1)} %fusion.9) | copy-start | bytes 294916
  591.5 0.7 copy-start.13
  591.6 162.4 %copy-start.3 = (bf16[64,768]{1,0:T(8,128)(2,1)S(1)}, bf16[64,768]{1,0:T(8,128)(2,1)}, u32[]{:S(2)}) copy-start(bf16[64,768]{1,0:T(8,128)(2,1)} %param.17) | copy-start | bytes 294916
  591.6 162.4 %copy-start.6 = (f32[768]{0:T(1024)S(1)}, f32[768]{0:T(1024)}, u32[]{:S(2)}) copy-start(f32[768]{0:T(1024)} %param.26) | copy-start | bytes 9220
  737.9 16.1 %all-to-all-start = ((bf16[8,8,768]{2,0,1:T(8,128)(2,1)}), bf16[8,8,768]{2,0,1:T(8,128)(2,1)S(1)}, u32[]{:S(2)}, u32[]{:S(2)}) async-start(bf16[8,8,768]{2,0,1:T(8,128)(2,1)} %bitcast.49), calls=%async_computation.2 | async-start | bytes 196608 | tf_op jit(solution)/shard_map/all_to_all | solution.py:163
Sparse Core Ops, SparseCore 0:
  42.2 63.6 all-gather.3
  117.3 145.6 reduce-scatter.2
  265.9 237.5 all-gather.7
  506.4 78.9 all-gather.5
  591.7 146.1 reduce-scatter.4
where the time goes:
time: 762 us; the launch traced here: 761 us
  waiting for transfers between devices  515 us (68%)
  blocking collectives  173 us (23%)
  matrix products  29.5 us (4%)
  between operations  14.1 us (2%)
  other arithmetic  11.6 us (2%)
  local copies, waits for them, and re-layouts  10.9 us (1%)
    reduce_scatter x1, waiting for transfers between devices, local(): lax.psum_scatter(jnp.concatenate([jnp.dot(attn_part, qkv_weight, preferre...  143 us
    reduce_scatter x1, waiting for transfers between devices, local(): lax.psum_scatter((jnp.dot(attn_part, full_out, preferred_element_type=jnp...  142 us
    all_gather x1, waiting for transfers between devices, local(): lax.all_gather(w_down, 'narrow', axis=1, tiled=True)  86.6 us
    all_gather x1, blocking collectives, local(): lax.all_gather(keys_local, 'narrow', axis=0, tiled=True)  76 us
    all_gather x1, waiting for transfers between devices, local(): lax.all_gather(w_attn_out, 'narrow', axis=1, tiled=True)  70.8 us
    all_gather x1, blocking collectives, local(): lax.all_gather(values_local, 'narrow', axis=0, tiled=True)  65.6 us
    all_gather x1, waiting for transfers between devices, local(): lax.all_gather(stacked, 'wide', axis=2, tiled=True)  63.7 us
    psum x1, blocking collectives, local(): total_sum, total_square = lax.psum((partial_sum, partial_square), 'narrow')  31.2 us
  transfers between devices with their start and end apart: 6, of which 6 were waited for; matrix products, arithmetic and copies ran while one was open for 4% of the time, Pallas kernels for 0%

commit v1 on v0

--- a/solution.py
+++ b/solution.py
@@ -78,9 +78,9 @@
     attn_normed = (scaled * norm_gain[0] + norm_bias[0]).astype(jnp.bfloat16)
     mlp_normed = (scaled * norm_gain[1] + norm_bias[1]).astype(jnp.bfloat16)
     stacked = jnp.stack([attn_normed, mlp_normed]).reshape(2, narrow_count, sub_rows, feat_local)
-    gathered = lax.all_gather(stacked, "wide", axis=2, tiled=True).reshape(
-        2, total_tokens, feat_local
-    )
+    gathered = jnp.concatenate(
+        lax.all_to_all(jnp.stack([stacked] * lax.axis_size("wide")), "wide", 0, 0), axis=2
+    ).reshape(2, total_tokens, feat_local)
     local_order = jnp.arange(query_rows, dtype=jnp.int32)
     local_tokens = (
         local_order // sub_rows * tok_local + narrow_index * sub_rows + local_order % sub_rows

time: 762 us -> 832 us (1.092)
  blocking collectives: 173 us -> 336 us
  waiting for transfers between devices: 515 us -> 429 us
    all_to_all x0 -> x1, blocking collectives: none -> 146 us  [local(): lax.all_to_all(jnp.stack([stacked] * lax.axis_size('wide')), 'wide', 0, 0)]
    all_gather x1 -> x0, waiting for transfers between devices: 63.7 us -> none  [local(): lax.all_gather(stacked, 'wide', axis=2, tiled=True)]
    all_gather x1, blocking collectives: 65.6 us -> 87.6 us  [local(): lax.all_gather(values_local, 'narrow', axis=0, tiled=True)]
    all_gather x1, waiting for transfers between devices: 86.6 us -> 69.4 us  [local(): lax.all_gather(w_down, 'narrow', axis=1, tiled=True)]
  transfers between devices with their start and end apart: 6 -> 5, of which waited for: 6 -> 5; matrix products, arithmetic and copies ran while one was open for 4% -> 3% of each run, Pallas kernels for 0% -> 0%
where the time goes in v1:
time: 832 us
  waiting for transfers between devices  429 us (52%)
  blocking collectives  336 us (40%)
  matrix products  26.6 us (3%)
  between operations  14.1 us (2%)
  other arithmetic  9.74 us (1%)
  local copies, waits for them, and re-layouts  8.81 us (1%)
    all_to_all x1, blocking collectives, local(): lax.all_to_all(jnp.stack([stacked] * lax.axis_size('wide')), 'wide', 0, 0)  146 us
    reduce_scatter x1, waiting for transfers between devices, local(): lax.psum_scatter((jnp.dot(attn_part, full_out, preferred_element_type=jnp...  142 us
    reduce_scatter x1, waiting for transfers between devices, local(): lax.psum_scatter(jnp.concatenate([jnp.dot(attn_part, qkv_weight, preferre...  138 us
    all_gather x1, blocking collectives, local(): lax.all_gather(values_local, 'narrow', axis=0, tiled=True)  87.6 us
    all_gather x1, blocking collectives, local(): lax.all_gather(keys_local, 'narrow', axis=0, tiled=True)  71.4 us
    all_gather x1, waiting for transfers between devices, local(): lax.all_gather(w_attn_out, 'narrow', axis=1, tiled=True)  70.1 us
    all_gather x1, waiting for transfers between devices, local(): lax.all_gather(w_down, 'narrow', axis=1, tiled=True)  69.4 us
    psum x1, blocking collectives, local(): total_sum, total_square = lax.psum((partial_sum, partial_square), 'narrow')  31.2 us
  transfers between devices with their start and end apart: 5, of which 5 were waited for; matrix products, arithmetic and copies ran while one was open for 3% of the time, Pallas kernels for 0%

profile of v1, /device:TPU:8, one launch (start us, length us, event | category | flops | bytes accessed | tf_op | source)
XLA Modules:
  0.0 831.7 jit_solution(15823747630921971396)
XLA Ops:
  7.2 1.1 convert_reduce_fusion
  8.3 31.2 %all-reduce = (f32[64]{0:T(128)S(1)}, f32[64]{0:T(128)S(1)}) all-reduce(f32[64]{0:T(128)S(1)} %get-tuple-element.4, f32[64]{0:T(128)S(1)} %get-tuple-element.3), channel_id=1, replica_groups=mesh['wide'=32,'narrow'=8] {'narrow'}, use_global_device_ids=true, to_apply=%region_3.0 | all-reduce | flops 128 | bytes 1024 | tf_op jit(solution)/shard_map/psum | solution.py:74
  39.6 0.8 slice_reduce_fusion.2
  40.4 1.0 fusion.72
  41.4 0.8 stack.18
  42.2 146.2 %all_to_all.18 = bf16[32,2,8,8,768]{4,3,2,1,0:T(8,128)(2,1)S(1)} all-to-all(bf16[32,2,8,8,768]{4,3,2,1,0:T(8,128)(2,1)S(1)} %stack.18), channel_id=1, replica_groups=mesh['wide'=32,'narrow'=8] {'wide'}, dimensions={0} | all-to-all | bytes 12582912 | tf_op jit(solution)/shard_map/all_to_all | solution.py:82
  188.4 0.6 copy.32
  189.5 2.9 convolution_convert_fusion
  192.4 2.0 convolution_convert_fusion.1
  194.5 2.9 pad_maximum_fusion
  197.5 0.7 all-gather.5.cloned.1.call-update
  198.2 0.7 all-gather.3.cloned.1.call-update
  199.6 0.9 fusion.6
  200.5 138.3 %reduce-scatter.3.cloned.1.call-done = bf16[256,1344]{0,1:T(8,128)(2,1)} async-done(((bf16[2048,1344]{0,1:T(8,128)(2,1)}), bf16[256,1344]{0,1:T(8,128)(2,1)}) %reduce-scatter.3.cloned.1.call-update) | async-done | bytes 688144 | tf_op jit(solution)/shard_map/reduce_scatter | solution.py:99
  338.8 1.2 convert_element_type.65
  340.0 1.1 copy-done.3
  341.4 71.4 %all_gather.13 = bf16[2048,192]{1,0:T(8,128)(2,1)S(1)} all-gather(bf16[256,192]{1,0:T(8,128)(2,1)S(1)} %copy.28), channel_id=1, replica_groups=mesh['wide'=32,'narrow'=8] {'narrow'}, dimensions={0}, use_global_device_ids=true | all-gather | bytes 884736 | tf_op jit(solution)/shard_map/all_gather | solution.py:122
  413.3 1.7 fusion.144
  415.1 87.6 %all_gather.12 = bf16[2048,192]{0,1:T(8,128)(2,1)S(1)} all-gather(bf16[256,192]{0,1:T(8,128)(2,1)S(1)} %get-tuple-element.24), channel_id=1, replica_groups=mesh['wide'=32,'narrow'=8] {'narrow'}, dimensions={0}, use_global_device_ids=true | all-gather | bytes 884736 | tf_op jit(solution)/shard_map/all_gather | solution.py:123
  502.6 2.7 fusion.9
  505.4 69.4 %all-gather.5.cloned.1.call-done = bf16[768,6144]{1,0:T(8,128)(2,1)} async-done(((bf16[768,768]{1,0:T(8,128)(2,1)}), bf16[768,6144]{1,0:T(8,128)(2,1)}) %all-gather.5.cloned.1.call-update) | async-done | bytes 9437200 | tf_op jit(solution)/shard_map/all_gather | solution.py:151
  574.8 11.0 %fusion.27 = f32[256,6144]{1,0:T(8,128)} fusion(bf16[768,6144]{1,0:T(8,128)(2,1)} %all-gather.5.cloned.1.call-done, f32[256,1344]{0,1:T(8,128)} %copy-done.3, f32[768]{0:T(1024)S(1)} %copy-done.12), kind=kOutput, calls=%fused_computation.47 | convolution fusion | flops 2428895232 | bytes 16518144 | tf_op jit(solution)/shard_map/dot_general | solution.py:157
  585.9 70.1 %all-gather.3.cloned.1.call-done = bf16[192,6144]{1,0:T(8,128)(2,1)} async-done(((bf16[192,768]{1,0:T(8,128)(2,1)}), bf16[192,6144]{1,0:T(8,128)(2,1)}) %all-gather.3.cloned.1.call-update) | async-done | bytes 2359312 | tf_op jit(solution)/shard_map/all_gather | solution.py:150
  655.9 6.2 fusion.1
  663.2 1.4 copy.30
  664.6 1.2 gather_fusion
  665.8 1.2 gather_fusion.1
  666.9 141.5 %reduce-scatter.5.cloned.1.call-done = bf16[8,6144]{1,0:T(8,128)(2,1)} async-done(((bf16[256,6144]{1,0:T(8,128)(2,1)}), bf16[8,6144]{1,0:T(8,128)(2,1)}) %reduce-scatter.5.cloned.1.call-update) | async-done | bytes 98320 | tf_op jit(solution)/shard_map/reduce_scatter | solution.py:154
  808.4 7.2 all-to-all-start.1
  815.7 0.7 pad_maximum_fusion.1
  816.5 8.0 all-to-all-done.1
  824.5 0.7 fusion.69
  (64 shorter events, 3.2 us)
Async XLA Ops:
  7.2 182.3 %copy-start = (bf16[768,768]{1,0:T(8,128)(2,1)S(1)}, bf16[768,768]{1,0:T(8,128)(2,1)}, u32[]{:S(2)}) copy-start(bf16[768,768]{1,0:T(8,128)(2,1)} %param.22) | copy-start | bytes 3538948
  7.2 331.6 %reduce-scatter.3.cloned.1.call-start = ((), (), s32[]{:S(2)}) async-start(), calls=%async_computation.4 | async-start | bytes 6193152 | tf_op jit(solution)/shard_map/reduce_scatter | solution.py:99
  189.4 3.0 copy-start.9
  189.5 3.0 copy-start.10
  189.5 3.0 copy-start.11
  197.4 1.6 copy-start.13
  197.4 1.8 copy-start.8
  197.4 2.0 copy-start.7
  197.4 377.4 %all-gather.5.cloned.1.call-start = ((), (), s32[]{:S(2)}) async-start(), calls=%async_computation.6 | async-start | bytes 10616832 | tf_op jit(solution)/shard_map/all_gather | solution.py:151
  198.2 457.8 %all-gather.3.cloned.1.call-start = ((), (), s32[]{:S(2)}) async-start(), calls=%async_computation.5 | async-start | bytes 2654208 | tf_op jit(solution)/shard_map/all_gather | solution.py:150
  198.9 609.5 %reduce-scatter.5.cloned.1.call-start = ((), (), s32[]{:S(2)}) async-start(), calls=%async_computation.7 | async-start | bytes 3244032 | tf_op jit(solution)/shard_map/reduce_scatter | solution.py:154
  340.0 1.1 copy-start.3
  341.3 73.8 %copy-start.5 = (bf16[256,2,12]{0,2,1:T(8,128)(2,1)}, bf16[256,2,12]{0,2,1:T(8,128)(2,1)S(1)}, u32[]{:S(2)}) copy-start(bf16[256,2,12]{0,2,1:T(8,128)(2,1)S(1)} %get-tuple-element.26) | copy-start | bytes 36868
  502.6 2.7 copy-start.2
  502.6 72.2 %copy-start.12 = (f32[768]{0:T(1024)S(1)}, f32[768]{0:T(1024)}, u32[]{:S(2)}) copy-start(f32[768]{0:T(1024)} %param.23) | copy-start | bytes 9220
  662.1 0.7 copy-start.14
  662.1 162.4 %copy-start.4 = (bf16[64,768]{1,0:T(8,128)(2,1)S(1)}, bf16[64,768]{1,0:T(8,128)(2,1)}, u32[]{:S(2)}) copy-start(bf16[64,768]{1,0:T(8,128)(2,1)} %param.17) | copy-start | bytes 294916
  662.1 162.4 %copy-start.6 = (f32[768]{0:T(1024)S(1)}, f32[768]{0:T(1024)}, u32[]{:S(2)}) copy-start(f32[768]{0:T(1024)} %param.26) | copy-start | bytes 9220
  662.2 163.0 %copy-start.1 = (bf16[768,768]{1,0:T(8,128)(2,1)S(1)}, bf16[768,768]{1,0:T(8,128)(2,1)}, u32[]{:S(2)}) copy-start(bf16[768,768]{1,0:T(8,128)(2,1)} %param.22) | copy-start | bytes 3538948
  808.4 16.1 %all-to-all-start.1 = ((bf16[8,8,768]{2,0,1:T(8,128)(2,1)}), bf16[8,8,768]{2,0,1:T(8,128)(2,1)S(1)}, u32[]{:S(2)}, u32[]{:S(2)}) async-start(bf16[8,8,768]{2,0,1:T(8,128)(2,1)} %bitcast.55), calls=%async_computation.3 | async-start | bytes 196608 | tf_op jit(solution)/shard_map/all_to_all | solution.py:163
Sparse Core Ops, SparseCore 0:
  197.5 141.1 reduce-scatter.2
  341.7 233.0 all-gather.4
  577.8 78.0 all-gather.2
  662.3 146.1 reduce-scatter.4
